TPU v7x, 32 devices: a whole 2x2x4 slice. The times are simulated.
32 devices in a mesh: dp: 8 (over y, x, core), hid: 4 (over z).
Axes of the slice: x: 2, y: 2, z: 4, core: 2. Of those that a mesh axis runs over, the one named last changes fastest.
Arguments:
- tokens: bfloat16 [4096, 8192], P('dp', 'hid'), may hold values from -6 to 6
- up_blocks: bfloat16 [7, 64, 128, 1024], P(None, 'hid', 'dp'), may hold values from -0.1875 to 0.1875
- up_left: bfloat16 [8192, 512], P('hid'), may hold values from -0.0625 to 0.0625
- up_right: bfloat16 [512, 65536], P(None, 'hid'), may hold values from -0.25 to 0.25
- down_blocks: bfloat16 [7, 64, 1024, 128], P(None, 'hid', 'dp'), may hold values from -0.0625 to 0.0625
- down_left: bfloat16 [65536, 512], P('hid'), may hold values from -0.0234375 to 0.0234375
- down_right: bfloat16 [512, 8192], P(None, 'hid'), may hold values from -0.25 to 0.25
Outputs:
- mixed: bfloat16 [4096, 8192], P('dp', 'hid')
All inputs are finite; a program needn't handle non-finite values.
Results may differ from a plain program's by a relative error of at most 0.0059.
Values may be sent and summed in bfloat16 or wider, within the bound.
A program may use at most 384 MiB of HBM per device.

v0:
```python
import jax
import jax.numpy as jnp
from jax import lax
from jax.sharding import PartitionSpec as P


def from_partner(block, axis, stride):
    count = lax.axis_size(axis)
    route = []
    for low in range(count):
        high = low | 1 << stride
        if high != low and high < count:
            route += [(low, high), (high, low)]
    return lax.ppermute(block, axis, route)


def swap_blocks(values, block_span, along_axis):
    full_shape = values.shape
    extent = full_shape[along_axis]
    split_shape = (
        full_shape[:along_axis]
        + (extent // (2 * block_span), 2, block_span)
        + full_shape[along_axis + 1 :]
    )
    return jnp.flip(values.reshape(split_shape), along_axis + 1).reshape(full_shape)


def shards(tokens, up_blocks, up_left, up_right, down_blocks, down_left, down_right):
    token_rows = tokens.shape[0]
    local_blocks = up_blocks.shape[1]
    block_size = down_blocks.shape[3]
    term_count = up_blocks.shape[0]
    pieces = tokens.reshape(token_rows, local_blocks, block_size)
    sources = []
    for step_index in range(term_count):
        block_span = 0 if step_index == 0 else 2 ** (step_index - 1)
        if block_span == 0:
            sources.append(pieces)
        elif block_span < local_blocks:
            sources.append(swap_blocks(pieces, block_span, 1))
        else:
            swap_bit = (block_span // local_blocks).bit_length() - 1
            partner_rows = from_partner(tokens, "hid", swap_bit)
            sources.append(partner_rows.reshape(token_rows, local_blocks, block_size))
    stacked = jnp.stack(sources)
    up_full = lax.all_gather(up_blocks, "dp", axis=2, tiled=True)
    hidden_sum = jnp.einsum("tabk,tbkn->abn", stacked, up_full, preferred_element_type=jnp.float32)
    down_full = lax.all_gather(down_blocks, "dp", axis=2, tiled=True)
    rank_up = lax.psum(jnp.dot(tokens, up_left, preferred_element_type=jnp.float32), "hid").astype(
        jnp.bfloat16
    )
    pre_activation = hidden_sum.reshape(
        token_rows, hidden_sum.shape[1] * hidden_sum.shape[2]
    ) + jnp.dot(rank_up, up_right, preferred_element_type=jnp.float32)
    active = jax.nn.gelu(pre_activation, approximate=False).astype(jnp.bfloat16)
    grouped = active.reshape(token_rows, local_blocks, hidden_sum.shape[2])
    contributions = jnp.einsum(
        "abn,tbnk->tabk", grouped, down_full, preferred_element_type=jnp.float32
    )
    out_sum = jnp.zeros((token_rows, local_blocks, block_size), jnp.float32)
    for step_index in range(term_count):
        block_span = 0 if step_index == 0 else 2 ** (step_index - 1)
        if block_span == 0:
            out_sum = contributions[0]
        elif block_span < local_blocks:
            out_sum = out_sum + swap_blocks(contributions[step_index], block_span, 1)
        else:
            swap_bit = (block_span // local_blocks).bit_length() - 1
            out_sum = out_sum + from_partner(contributions[step_index], "hid", swap_bit)
    rank_down = lax.psum(
        jnp.dot(active, down_left, preferred_element_type=jnp.float32), "hid"
    ).astype(jnp.bfloat16)
    result = out_sum.reshape(token_rows, local_blocks * block_size) + jnp.dot(
        rank_down, down_right, preferred_element_type=jnp.float32
    )
    return result.astype(jnp.bfloat16)


def solution(mesh):
    placed = (
        P("dp", "hid"),
        P(None, "hid", "dp", None),
        P("hid", None),
        P(None, "hid"),
        P(None, "hid", "dp", None),
        P("hid", None),
        P(None, "hid"),
    )
    return jax.shard_map(
        shards, mesh=mesh, in_specs=placed, out_specs=P("dp", "hid"), check_vma=False
    )
```

profile of v0, /device:TPU:0, one launch (start us, length us, event | category | flops | bytes accessed | tf_op | source)
XLA Modules:
  0.0 731.6 jit_solution(11911932797676576701)
XLA Ops:
  6.5 4.7 copy.28
  11.3 6.1 copy.31
  17.4 3.9 copy.18
  27.0 4.6 reshape_reshape.12
  31.6 4.5 reshape_reshape.13
  36.0 4.5 reshape_reshape.14
  40.5 3.9 copy.25
  44.4 3.4 copy.19
  51.0 3.4 copy.20
  71.4 4.2 fusion.25
  75.5 5.2 constant_dynamic-update-slice_fusion.6
  89.3 65.1 %all-reduce.2 = bf16[512,512]{1,0:T(8,128)(2,1)} all-reduce(f32[512,512]{1,0:T(8,128)S(1)} %fusion.25), channel_id=1, replica_groups=mesh['dp'=8,'hid'=4] {'hid'}, use_global_device_ids=true, to_apply=%region_0.1 | all-reduce | flops 262144 | bytes 1572864 | tf_op jit(solution)/shard_map/psum | solution.py:49
  154.3 4.1 copy.26
  158.5 3.9 copy.27
  165.8 3.9 constant_dynamic-update-slice_fusion
  169.7 31.9 %convolution_bitcast_fusion = f32[512,16,1024]{2,0,1:T(8,128)} fusion(bf16[7,512,16,128]{3,1,0,2:T(8,128)(2,1)} %constant_dynamic-update-slice_fusion, bf16[7,16,128,1024]{3,2,0,1:T(8,128)(2,1)} %all-gather.3.cloned.1.call-done), kind=kOutput, calls=%fused_computation.21 | convolution fusion | flops 15032385536 | bytes 77594624 | tf_op jit(solution)/shard_map/tabk,tbkn->abn/dot_general | solution.py:47
  201.6 32.2 %copy.29 = f32[512,16,1024]{0,2,1:T(8,128)} copy(f32[512,16,1024]{2,0,1:T(8,128)} %convolution_bitcast_fusion) | data formatting | bytes 67108864 | tf_op jit(solution)/shard_map/tabk,tbkn->abn/transpose | solution.py:47
  233.8 31.3 %copy.30 = f32[512,16384]{1,0:T(8,128)} copy(f32[512,16384]{0,1:T(8,128)} %bitcast.69) | data formatting | bytes 67108864 | tf_op jit(solution)/shard_map/reshape | solution.py:52
  265.1 82.0 %fusion.2 = bf16[512,16384]{1,0:T(8,128)(2,1)S(1)} fusion(f32[512,16384]{1,0:T(8,128)} %copy.30, bf16[512,16384]{1,0:T(8,128)(2,1)} %param.10, bf16[512,512]{1,0:T(8,128)(2,1)S(1)} %copy-done.5), kind=kOutput, calls=%fused_computation.3 | convolution fusion | flops 9143582720 | bytes 67633152 | tf_op jit(solution)/shard_map/dot_general | solution.py:54
  347.1 5.7 copy-done.1
  352.8 12.0 %copy.43 = bf16[64,8,16,1024]{3,2,1,0:T(8,128)(2,1)} copy(bf16[64,8,16,1024]{3,1,2,0:T(8,128)(2,1)S(1)} %bitcast.75) | data formatting | bytes 33554432
  364.8 91.9 %fusion.12 = f32[7,512,16,128]{1,3,0,2:T(8,128)} fusion(bf16[7,16,1024,128]{2,3,0,1:T(8,128)(2,1)} %all-gather.5.cloned.1.call-done, bf16[512,16,1024,1]{2,1,0,3:T(8,128)(2,1)} %bitcast.76), kind=kOutput, calls=%fused_computation.22 | convolution fusion | flops 15032385536 | bytes 75497472 | tf_op jit(solution)/shard_map/abn,tbnk->tabk/dot_general | solution.py:57
  456.8 17.7 %fusion.24 = (f32[1,512,16,128]{1,3,0,2:T(8,128)}, f32[512,16,128]{0,2,1:T(8,128)}, f32[1,512,16,128]{1,3,0,2:T(8,128)}, f32[1,512,16,128]{1,3,0,2:T(8,128)}, f3...) fusion(f32[7,512,16,128]{1,3,0,2:T(8,128)} %fusion.12), kind=kLoop, calls=%fused_computation.43 | loop fusion | bytes 50331648 | tf_op jit(solution)/shard_map/slice | solution.py:66
  477.1 4.8 rev.36
  481.9 4.7 rev.37
  486.6 4.7 rev.38
  491.4 4.8 rev.39
  496.2 18.1 %fusion.26 = f32[512,512]{1,0:T(8,128)} fusion(bf16[512,16384]{1,0:T(8,128)(2,1)} %copy-done.1, bf16[16384,512]{1,0:T(8,128)(2,1)} %param.12), kind=kOutput, calls=%fused_computation.45 | convolution fusion | flops 8589934592 | bytes 34603008 | tf_op jit(solution)/shard_map/dot_general | solution.py:71
  514.3 183.0 %all-reduce.3 = bf16[512,512]{1,0:T(8,128)(2,1)S(1)} all-reduce(f32[512,512]{1,0:T(8,128)} %fusion.26), channel_id=1, replica_groups=mesh['dp'=8,'hid'=4] {'hid'}, use_global_device_ids=true, to_apply=%region_1.2 | all-reduce | flops 262144 | bytes 1572864 | tf_op jit(solution)/shard_map/psum | solution.py:70
  700.5 13.4 %fusion.20 = f32[512,16,128]{0,2,1:T(8,128)} fusion(f32[512,16,128]{0,2,1:T(8,128)} %collective-permute-done.3, f32[512,16,128]{0,2,1:T(8,128)} %collective-permute-done.2, f32[7,512,16,128]{1,3,0,2:T(8,128)} %fusion.12, f32[512,1,2,8,128]{0,4,3,2,1:T(8,128)} %rev.39, f32[512,2,2,4,128]{0,4,3,2,1:T(8,128)} %rev.38, f32[512,4,2,2,128]{0,4,3,2,1:T(8,128)} %rev.37, ...), kind=kLoop, calls=%fused_computation.31 | loop fusion | flops 6291456 | bytes 33554432 | tf_op jit(solution)/shard_map/add | solution.py:69
  713.8 5.4 copy.35
  719.2 5.4 add_convert_fusion
  (38 shorter events, 43.6 us)
Async XLA Ops:
  6.5 690.7 %copy-start = (bf16[512,2048]{1,0:T(8,128)(2,1)S(1)}, bf16[512,2048]{1,0:T(8,128)(2,1)}, u32[]{:S(2)}) copy-start(bf16[512,2048]{1,0:T(8,128)(2,1)} %param.13) | copy-start | bytes 6291460
  6.5 163.1 %all-gather.3.cloned.1.call-start = ((), (), s32[]{:S(2)}) async-start(), calls=%async_computation | async-start | bytes 33030144 | tf_op jit(solution)/shard_map/all_gather | solution.py:46
  11.2 353.6 %all-gather.5.cloned.1.call-start = ((), (), s32[]{:S(2)}) async-start(), calls=%async_computation.1 | async-start | bytes 33030144 | tf_op jit(solution)/shard_map/all_gather | solution.py:48
  21.3 133.0 %collective-permute-start = (bf16[512,2048]{0,1:T(8,128)(2,1)}, bf16[512,2048]{0,1:T(8,128)(2,1)}, u32[]{:S(2)}, u32[]{:S(2)}) collective-permute-start(bf16[512,2048]{0,1:T(8,128)(2,1)} %copy.18), channel_id=1, source_target_pairs={{0,1},{1,0},{2,3},{3,2},{4,5},{5,4},{6,7},{7,6},{8,9},{9,8},{10,11... | collective-permute-start | bytes 6291464 | tf_op jit(solution)/shard_map/ppermute | solution.py:14
  24.4 134.1 %collective-permute-start.1 = (bf16[512,2048]{0,1:T(8,128)(2,1)}, bf16[512,2048]{0,1:T(8,128)(2,1)}, u32[]{:S(2)}, u32[]{:S(2)}) collective-permute-start(bf16[512,2048]{0,1:T(8,128)(2,1)} %copy.18), channel_id=1, source_target_pairs={{0,2},{2,0},{1,3},{3,1},{4,6},{6,4},{5,7},{7,5},{8,10},{10,8},{9,1... | collective-permute-start | bytes 6291464 | tf_op jit(solution)/shard_map/ppermute | solution.py:14
  71.3 12.8 %copy-start.2 = (bf16[512,4,2,2,128]{4,0,3,2,1:T(8,128)(2,1)S(1)}, bf16[512,4,2,2,128]{4,0,3,2,1:T(8,128)(2,1)}, u32[]{:S(2)}) copy-start(bf16[512,4,2,2,128]{4,0,3,2,1:T(8,128)(2,1)} %rev.33) | copy-start | bytes 6291460
  71.4 14.5 %copy-start.3 = (bf16[512,2,2,4,128]{4,0,3,2,1:T(8,128)(2,1)S(1)}, bf16[512,2,2,4,128]{4,0,3,2,1:T(8,128)(2,1)}, u32[]{:S(2)}) copy-start(bf16[512,2,2,4,128]{4,0,3,2,1:T(8,128)(2,1)} %rev.34) | copy-start | bytes 6291460
  71.4 16.2 %copy-start.4 = (bf16[512,1,2,8,128]{4,0,3,2,1:T(8,128)(2,1)S(1)}, bf16[512,1,2,8,128]{4,0,3,2,1:T(8,128)(2,1)}, u32[]{:S(2)}) copy-start(bf16[512,1,2,8,128]{4,0,3,2,1:T(8,128)(2,1)} %rev.35) | copy-start | bytes 6291460
  233.8 31.3 %copy-start.5 = (bf16[512,512]{1,0:T(8,128)(2,1)S(1)}, bf16[512,512]{1,0:T(8,128)(2,1)}, u32[]{:S(2)}) copy-start(bf16[512,512]{1,0:T(8,128)(2,1)} %all-reduce.2) | copy-start | bytes 1572868
  347.1 5.7 copy-start.1
  474.5 226.0 %collective-permute-start.2 = (f32[512,16,128]{0,2,1:T(8,128)}, f32[512,16,128]{0,2,1:T(8,128)}, u32[]{:S(2)}, u32[]{:S(2)}) collective-permute-start(f32[512,16,128]{0,2,1:T(8,128)} %get-tuple-element.10), channel_id=1, source_target_pairs={{0,1},{1,0},{2,3},{3,2},{4,5},{5,4},{6,7},{7,6},{8,9},{9,8},{10,11... | collective-permute-start | bytes 12582920 | tf_op jit(solution)/shard_map/ppermute | solution.py:14
  474.7 225.8 %collective-permute-start.3 = (f32[512,16,128]{0,2,1:T(8,128)}, f32[512,16,128]{0,2,1:T(8,128)}, u32[]{:S(2)}, u32[]{:S(2)}) collective-permute-start(f32[512,16,128]{0,2,1:T(8,128)} %get-tuple-element.6), channel_id=1, source_target_pairs={{0,2},{2,0},{1,3},{3,1},{4,6},{6,4},{5,7},{7,5},{8,10},{10,8},{9,1... | collective-permute-start | bytes 12582920 | tf_op jit(solution)/shard_map/ppermute | solution.py:14
Sparse Core Ops, SparseCore 0:
  11.3 145.7 all-gather.2
  159.0 148.8 all-gather.4
where the time goes:
time: 740 us; the launch traced here: 732 us
  blocking collectives  248 us (34%)
  matrix products  231 us (31%)
  local copies, waits for them, and re-layouts  211 us (29%)
  other arithmetic  18.8 us (3%)
  between operations  13.7 us (2%)
  starting transfers between devices  8.36 us (1%)
    psum x1, blocking collectives, shards(): lax.psum(jnp.dot(active, down_left, preferred_element_type=jnp.float32),...  183 us
    dot_general x1, matrix products, shards(): jnp.einsum('abn,tbnk->tabk', grouped, down_full, preferred_element_type=j...  91.9 us
    dot_general x1, matrix products, shards(): jnp.dot(rank_up, up_right, preferred_element_type=jnp.float32)  82 us
    psum x1, blocking collectives, shards(): lax.psum(jnp.dot(tokens, up_left, preferred_element_type=jnp.float32), 'h...  65.1 us
    unnamed x23, local copies, waits for them, and re-layouts  51.8 us
    transpose x1, local copies, waits for them, and re-layouts, shards(): jnp.einsum('tabk,tbkn->abn', stacked, up_full, preferred_element_type=jnp...  32.2 us
    dot_general x1, matrix products, shards(): jnp.einsum('tabk,tbkn->abn', stacked, up_full, preferred_element_type=jnp...  31.9 us
    rev x8, local copies, waits for them, and re-layouts, swap_blocks(): jnp.flip(values.reshape(split_shape), along_axis + 1).reshape(full_shape)  31.6 us
  transfers between devices with their start and end apart: 6, of which 0 were waited for; matrix products, arithmetic and copies ran while one was open for 43% of the time, Pallas kernels for 0%

commit v1 on v0

--- a/solution.py
+++ b/solution.py
@@ -1,6 +1,10 @@
+import functools
+
 import jax
 import jax.numpy as jnp
 from jax import lax
+from jax.experimental import pallas as pl
+from jax.experimental.pallas import tpu as pltpu
 from jax.sharding import PartitionSpec as P
 
 
@@ -25,7 +29,7 @@
     return jnp.flip(values.reshape(split_shape), along_axis + 1).reshape(full_shape)
 
 
-def shards(tokens, up_blocks, up_left, up_right, down_blocks, down_left, down_right):
+def shards_plain(tokens, up_blocks, up_left, up_right, down_blocks, down_left, down_right):
     token_rows = tokens.shape[0]
     local_blocks = up_blocks.shape[1]
     block_size = down_blocks.shape[3]
@@ -76,6 +80,366 @@
     return result.astype(jnp.bfloat16)
 
 
+GROUPS = 2
+AHEAD = 4
+MESH = pl.DeviceIdType.MESH
+
+
+def flip(index, bit):
+    return index + bit - 2 * bit * ((index // bit) % 2)
+
+
+def fused(
+    tokens, up_blocks, up_left, up_right, down_blocks, down_left, down_right,
+    out, up_all, down_all,
+    tok, swapped, left, right, rank, rank_part, rank_in, active, acc, give, take,
+    w_up, w_right, w_down, w_left,
+    sent, got, tok_sent, tok_got, give_sent, give_got,
+    rs_sent, rs_got, ag_sent, ag_got, own_sem, load_sem, pre_sem,
+):
+    rows = tokens.shape[0]
+    terms, blocks = up_blocks.shape[0], up_blocks.shape[1]
+    size = down_blocks.shape[3]
+    width = up_blocks.shape[3]
+    depth = terms * size
+    units = blocks // GROUPS
+    me, here = lax.axis_index("dp"), lax.axis_index("hid")
+    slabs = lax.axis_size("hid")
+    bits = slabs.bit_length() - 1
+    locals_ = terms - bits
+    share = rows // slabs
+    sibling, across, beside = flip(me, 1), flip(me, 2), flip(me, 4)
+    chunk = GROUPS * size
+
+    barrier = pltpu.get_barrier_semaphore()
+    for near in (sibling, across, beside):
+        pl.semaphore_signal(barrier, inc=1, device_id=(near, here), device_id_type=MESH)
+    for k in range(1, slabs):
+        pl.semaphore_signal(
+            barrier, inc=1, device_id=(me, (here + k) % slabs), device_id_type=MESH
+        )
+    pl.semaphore_wait(barrier, 3 + slabs - 1)
+
+    stages = ((up_blocks, up_all), (down_blocks, down_all))
+
+    def remote(source, target, send, recv, device):
+        return pltpu.make_async_remote_copy(
+            src_ref=source, dst_ref=target, send_sem=send, recv_sem=recv,
+            device_id=device, device_id_type=MESH,
+        )
+
+    def hop(stage, kind, unit):
+        blocks_ref, all_ref = stages[stage]
+        span = pl.ds(unit * GROUPS, GROUPS)
+        odd = unit % 2
+        if kind < 3:
+            source, slot = blocks_ref.at[:, span], me
+            target = (sibling, across, beside)[kind]
+        elif kind == 3:
+            slot, target = across, sibling
+        elif kind == 4:
+            slot, target = beside, sibling
+        elif kind == 5:
+            slot = across * (1 - odd) + beside * odd
+            target = beside * (1 - odd) + across * odd
+        else:
+            slot, target = flip(across, 4), sibling
+        place = all_ref.at[:, span, slot]
+        if kind >= 3:
+            source = place
+        return remote(source, place, sent.at[stage, kind, unit], got.at[stage, kind, unit], (target, here))
+
+    def own(stage, unit):
+        blocks_ref, all_ref = stages[stage]
+        span = pl.ds(unit * GROUPS, GROUPS)
+        return pltpu.make_async_copy(
+            blocks_ref.at[:, span], all_ref.at[:, span, me], own_sem.at[stage, unit]
+        )
+
+    def direct(stage, unit):
+        for kind in (1, 2, 0):
+            hop(stage, kind, unit).start()
+        own(stage, unit).start()
+
+    def forward(stage, unit):
+        hop(stage, 1, unit).wait_recv()
+        hop(stage, 2, unit).wait_recv()
+        for kind in (5, 3, 4):
+            hop(stage, kind, unit).start()
+
+    def relay(stage, unit):
+        hop(stage, 5, unit).wait_recv()
+        hop(stage, 6, unit).start()
+
+    def settle(stage, unit):
+        for kind in (0, 3, 4, 6):
+            hop(stage, kind, unit).wait_recv()
+        own(stage, unit).wait()
+
+    def advance(unit, stage):
+        for step, action in ((AHEAD, direct), (2, forward), (1, relay)):
+            if stage == 1:
+                pl.when(unit + step < units)(functools.partial(action, 1, unit + step))
+            else:
+                pl.when(unit + step < units)(functools.partial(action, 0, unit + step))
+                pl.when(unit + step >= units)(functools.partial(action, 1, unit + step - units))
+        settle(stage, unit)
+
+    def swap(bit, unit):
+        cols = pl.ds(pl.multiple_of(unit * chunk, chunk), chunk)
+        return remote(
+            tokens.at[:, cols], swapped.at[bit, :, cols],
+            tok_sent.at[bit, unit], tok_got.at[bit, unit], (me, flip(here, 1 << bit)),
+        )
+
+    def hand(bit, unit):
+        cols = pl.ds(pl.multiple_of(unit * chunk, chunk), chunk)
+        return remote(
+            give.at[bit, :, cols], take.at[bit, :, cols],
+            give_sent.at[bit, unit], give_got.at[bit, unit], (me, flip(here, 1 << bit)),
+        )
+
+    def scatter(which, k):
+        there = (here + k) % slabs
+        return remote(
+            rank_part.at[which, pl.ds(pl.multiple_of(there * share, share), share)],
+            rank_in.at[which, k - 1],
+            rs_sent.at[which, k - 1], rs_got.at[which, k - 1], (me, there),
+        )
+
+    def gather(which, k):
+        there = (here + k) % slabs
+        mine = rank.at[which, pl.ds(pl.multiple_of(here * share, share), share)]
+        return remote(mine, mine, ag_sent.at[which, k - 1], ag_got.at[which, k - 1], (me, there))
+
+    def add_shares(which):
+        for k in range(1, slabs):
+            scatter(which, k).wait_recv()
+        mine = pl.ds(pl.multiple_of(here * share, share), share)
+        total = rank_part[which, mine, :]
+        for k in range(1, slabs):
+            total = total + rank_in[which, k - 1]
+        rank[which, mine, :] = total.astype(jnp.bfloat16)
+        for k in range(1, slabs):
+            gather(which, k).start()
+
+    pre = [
+        pltpu.make_async_copy(source, target, pre_sem.at[i])
+        for i, (source, target) in enumerate(((tokens, tok), (up_left, left), (down_right, right)))
+    ]
+    for copy in pre[:2]:
+        copy.start()
+    for unit in range(AHEAD):
+        direct(0, unit)
+    pre[2].start()
+    for copy in pre[:2]:
+        copy.wait()
+    rank_part[0, :, :] = jnp.dot(tok[...], left[...], preferred_element_type=jnp.float32)
+    for k in range(1, slabs):
+        scatter(0, k).start()
+    for unit in range(2):
+        for bit in range(bits):
+            swap(bit, unit).start()
+    acc[...] = jnp.zeros_like(acc)
+    rank_part[1, :, :] = jnp.zeros_like(rank_part[1])
+    forward(0, 0)
+    add_shares(0)
+    for unit in range(2, units):
+        for bit in range(bits):
+            swap(bit, unit).start()
+    relay(0, 0)
+    forward(0, 1)
+    for k in range(1, slabs):
+        gather(0, k).wait_recv()
+
+    tile = 256
+
+    def up_unit(unit, carry):
+        advance(unit, 0)
+        loads = []
+        for j in range(GROUPS):
+            group = unit * GROUPS + j
+            span = pl.ds(pl.multiple_of(group * width, width), width)
+            loads.append((
+                pltpu.make_async_copy(up_all.at[:, group], w_up.at[j], load_sem.at[0, j]),
+                pltpu.make_async_copy(up_right.at[:, span], w_right.at[j], load_sem.at[1, j]),
+                pltpu.make_async_copy(down_left.at[span], w_left.at[j], load_sem.at[2, j]),
+            ))
+        for trio in loads:
+            for copy in trio:
+                copy.start()
+        for bit in range(bits):
+            swap(bit, unit).wait_recv()
+        for j in range(GROUPS):
+            group = unit * GROUPS + j
+            for copy in loads[j]:
+                copy.wait()
+            parts = []
+            for term in range(terms):
+                if term == 0:
+                    at = group
+                elif term < locals_:
+                    at = flip(group, 1 << (term - 1))
+                else:
+                    at = group
+                cols = pl.ds(pl.multiple_of(at * size, size), size)
+                parts.append(tok[:, cols] if term < locals_ else swapped[term - locals_, :, cols])
+            source = jnp.concatenate(parts, axis=1)
+            coords = rank[0]
+            for n in range(width // tile):
+                cut = slice(n * tile, (n + 1) * tile)
+                weights = w_up[j, :, :, :, cut].reshape(depth, tile)
+                pre_act = jnp.dot(source, weights, preferred_element_type=jnp.float32)
+                pre_act += jnp.dot(coords, w_right[j, :, cut], preferred_element_type=jnp.float32)
+                value = 0.5 * pre_act * (1.0 + lax.erf(pre_act * (0.5 ** 0.5)))
+                start = pl.multiple_of(group * width + n * tile, tile)
+                active[:, pl.ds(start, tile)] = value.astype(jnp.bfloat16)
+            span = pl.ds(pl.multiple_of(group * width, width), width)
+            rank_part[1, :, :] += jnp.dot(
+                active[:, span], w_left[j], preferred_element_type=jnp.float32
+            )
+        return carry
+
+    lax.fori_loop(0, units, up_unit, 0)
+    for k in range(1, slabs):
+        scatter(1, k).start()
+    pre[2].wait()
+
+    def down_unit(unit, carry):
+        advance(unit, 1)
+        loads = [
+            pltpu.make_async_copy(
+                down_all.at[:, unit * GROUPS + j], w_down.at[j], load_sem.at[0, j]
+            )
+            for j in range(GROUPS)
+        ]
+        for copy in loads:
+            copy.start()
+        pl.when(unit == 2)(functools.partial(add_shares, 1))
+
+        @pl.when(unit == 5)
+        def _():
+            for k in range(1, slabs):
+                gather(1, k).wait_recv()
+            for n in range(acc.shape[1] // 512):
+                cut = slice(n * 512, (n + 1) * 512)
+                acc[:, cut] += jnp.dot(rank[1], right[:, cut], preferred_element_type=jnp.float32)
+
+        for j in range(GROUPS):
+            group = unit * GROUPS + j
+            loads[j].wait()
+            span = pl.ds(pl.multiple_of(group * width, width), width)
+            source = active[:, span]
+            for first in range(0, terms, 2):
+                pair = range(first, min(first + 2, terms))
+                weights = jnp.concatenate(
+                    [w_down[j, term].reshape(width, size) for term in pair], axis=1
+                )
+                product = jnp.dot(source, weights, preferred_element_type=jnp.float32)
+                for term in pair:
+                    piece = product[:, (term - first) * size : (term - first + 1) * size]
+                    if term < locals_:
+                        at = group if term == 0 else flip(group, 1 << (term - 1))
+                        acc[:, pl.ds(pl.multiple_of(at * size, size), size)] += piece
+                    else:
+                        cols = pl.ds(pl.multiple_of(group * size, size), size)
+                        give[term - locals_, :, cols] = piece.astype(jnp.bfloat16)
+        for bit in range(bits):
+            hand(bit, unit).start()
+        return carry
+
+    lax.fori_loop(0, units, down_unit, 0)
+
+    def finish(unit, carry):
+        cols = pl.ds(pl.multiple_of(unit * chunk, chunk), chunk)
+        for bit in range(bits):
+            hand(bit, unit).wait_recv()
+        total = acc[:, cols]
+        for bit in range(bits):
+            total = total + take[bit, :, cols].astype(jnp.float32)
+        out[:, cols] = total.astype(jnp.bfloat16)
+        for stage in range(2):
+            for kind in range(7):
+                hop(stage, kind, unit).wait_send()
+        for bit in range(bits):
+            swap(bit, unit).wait_send()
+            hand(bit, unit).wait_send()
+        return carry
+
+    lax.fori_loop(0, units, finish, 0)
+    for which in range(2):
+        for k in range(1, slabs):
+            scatter(which, k).wait_send()
+            gather(which, k).wait_send()
+
+
+def shards_fused(tokens, up_blocks, up_left, up_right, down_blocks, down_left, down_right):
+    rows, features = tokens.shape
+    terms, blocks, up_rows, width = up_blocks.shape
+    down_rows, size = down_blocks.shape[2:]
+    rank = up_left.shape[1]
+    count, slabs = lax.axis_size("dp"), lax.axis_size("hid")
+    bits = slabs.bit_length() - 1
+    units = blocks // GROUPS
+    any_ = pl.BlockSpec(memory_space=pl.ANY)
+    bf, f32 = jnp.bfloat16, jnp.float32
+    dma = pltpu.SemaphoreType.DMA
+    out, _, _ = pl.pallas_call(
+        fused,
+        out_shape=(
+            jax.ShapeDtypeStruct((rows, features), bf),
+            jax.ShapeDtypeStruct((terms, blocks, count, up_rows, width), bf),
+            jax.ShapeDtypeStruct((terms, blocks, count, down_rows, size), bf),
+        ),
+        in_specs=[any_] * 7,
+        out_specs=(pl.BlockSpec(memory_space=pltpu.VMEM), any_, any_),
+        scratch_shapes=[
+            pltpu.VMEM((rows, features), bf),
+            pltpu.VMEM((bits, rows, features), bf),
+            pltpu.VMEM((features, rank), bf),
+            pltpu.VMEM((rank, features), bf),
+            pltpu.VMEM((2, rows, rank), bf),
+            pltpu.VMEM((2, rows, rank), f32),
+            pltpu.VMEM((2, slabs - 1, rows // slabs, rank), f32),
+            pltpu.VMEM((rows, blocks * width), bf),
+            pltpu.VMEM((rows, features), f32),
+            pltpu.VMEM((bits, rows, features), bf),
+            pltpu.VMEM((bits, rows, features), bf),
+            pltpu.VMEM((GROUPS, terms, count, up_rows, width), bf),
+            pltpu.VMEM((GROUPS, rank, width), bf),
+            pltpu.VMEM((GROUPS, terms, count, down_rows, size), bf),
+            pltpu.VMEM((GROUPS, width, rank), bf),
+            dma((2, 7, units)), dma((2, 7, units)),
+            dma((bits, units)), dma((bits, units)),
+            dma((bits, units)), dma((bits, units)),
+            dma((2, slabs - 1)), dma((2, slabs - 1)),
+            dma((2, slabs - 1)), dma((2, slabs - 1)),
+            dma((2, units)), dma((3, GROUPS)), dma((3,)),
+        ],
+        compiler_params=pltpu.CompilerParams(
+            collective_id=0, has_side_effects=True, vmem_limit_bytes=62 * 1024 * 1024
+        ),
+    )(tokens, up_blocks, up_left, up_right, down_blocks, down_left, down_right)
+    return out
+
+
+def shards(tokens, up_blocks, *rest):
+    terms, blocks, up_rows, _ = up_blocks.shape
+    slabs = lax.axis_size("hid")
+    reach = blocks.bit_length() - 1 + slabs.bit_length()
+    fits = (
+        lax.axis_size("dp") == 8
+        and up_rows % 16 == 0
+        and blocks >= GROUPS * 6
+        and blocks % GROUPS == 0
+        and terms == reach
+        and slabs > 1
+        and tokens.shape[0] % (16 * slabs) == 0
+    )
+    body = shards_fused if fits else shards_plain
+    return body(tokens, up_blocks, *rest)
+
+
 def solution(mesh):
     placed = (
         P("dp", "hid"),

time: 740 us -> 313 us (0.42); the launches traced: 732 us -> 313 us
  Pallas kernels: 0 us -> 310 us
  blocking collectives: 248 us -> 0 us
  matrix products: 231 us -> 0 us
  local copies, waits for them, and re-layouts: 211 us -> 3.16 us
  other arithmetic: 18.8 us -> 0 us
  between operations: 13.7 us -> 0.01 us
  starting transfers between devices: 8.36 us -> 0 us
    pallas_call x0 -> x1, Pallas kernels: none -> 310 us  [shards_fused(): pl.pallas_call(fused, out_shape=(jax.ShapeDtypeStruct((rows, features), b...]
    psum x2 -> x0, blocking collectives: 248 us -> none  [the longest x1 183 us: shards(): lax.psum(jnp.dot(active, down_left, preferred_element_type=jnp.float32),...]
    dot_general x6 -> x0, matrix products: 231 us -> none  [the longest x1 91.9 us: shards(): jnp.einsum('abn,tbnk->tabk', grouped, down_full, preferred_element_type=j...]
    unnamed x23 -> x1, local copies, waits for them, and re-layouts: 51.8 us -> 3.16 us
    another operation x11 -> x0, local copies, waits for them, and re-layouts: 41.5 us -> none  [the longest x7 25.7 us: swap_blocks(): values.reshape(split_shape)]
    reshape x2 -> x0, local copies, waits for them, and re-layouts: 36.7 us -> none  [the longest x1 31.3 us: shards(): hidden_sum.reshape(token_rows, hidden_sum.shape[1] * hidden_sum.shape[2])]
    transpose x1 -> x0, local copies, waits for them, and re-layouts: 32.2 us -> none  [shards(): jnp.einsum('tabk,tbkn->abn', stacked, up_full, preferred_element_type=jnp...]
    rev x8 -> x0, local copies, waits for them, and re-layouts: 31.6 us -> none  [swap_blocks(): jnp.flip(values.reshape(split_shape), along_axis + 1).reshape(full_shape)]
  transfers between devices with their start and end apart: 6 -> 0, of which waited for: 0 -> 0; matrix products, arithmetic and copies ran while one was open for 43% -> 0% of each run, Pallas kernels for 0% -> 0%
where the time goes in v1:
time: 313 us
  Pallas kernels  310 us (99%)
  local copies, waits for them, and re-layouts  3.16 us (1%)
    pallas_call x1, Pallas kernels, shards_fused(): pl.pallas_call(fused, out_shape=(jax.ShapeDtypeStruct((rows, features), b...  310 us

profile of v1, /device:TPU:0, one launch (start us, length us, event | category | flops | bytes accessed | tf_op | source)
XLA Modules:
  0.0 312.8 jit_solution(4710882028182844881)
XLA Ops:
  0.0 309.6 %shard_map.73 = (bf16[512,2048]{1,0:T(8,128)(2,1)}, bf16[7,16,8,16,1024]{4,3,2,1,0:T(8,128)(2,1)}, bf16[7,16,8,128,128]{4,3,2,1,0:T(8,128)(2,1)}) custom-call(bf16[512,2048]{1,0:T(8,128)(2,1)} %tokens.1, bf16[7,16,16,1024]{3,2,1,0:T(8,128)(2,1)} %up_blocks.1, bf16[2048,512]{1,0:T(8,128)(2,1)} %up_left.1, bf16[512,16384]{1,0:T(8,128)(2,1)} %up_right.1, ...), custom_call_target="tpu_custom_call" | custom-call | tf_op jit(solution)/shard_map/pallas_call | solution.py:387
  309.6 3.2 %copy.9 = bf16[512,2048]{1,0:T(8,128)(2,1)} copy(bf16[512,2048]{1,0:T(8,128)(2,1)} %get-tuple-element.6) | data formatting | bytes 4194304
